TPU v7x, 32 devices: a whole 2x2x4 slice. The times are simulated.
32 devices in a mesh: row: 16 (over z, y, x), col: 2 (over core).
Axes of the slice: x: 2, y: 2, z: 4, core: 2. Of those that a mesh axis runs over, the one named last changes fastest.
Arguments:
- sim_points: float32 [64, 4096], P(None, 'row'), may hold values from -34 to 34
- obs_points: float32 [64, 4096], P(None, ('row', 'col')), may hold values from -16 to 16
- sim_logw: float32 [4096], P('row'), may hold values from -2.5 to 2.5
- obs_logw: float32 [4096], P(('row', 'col')), may hold values from -2.5 to 2.5
Outputs:
- potential_f: float32 [4096], P('row')
- potential_g: float32 [4096], P(('row', 'col'))
- transport_cost: float32 [1], replicated
All inputs are finite; a program needn't handle non-finite values.
Results may differ from a plain program's by a relative error of at most 0.0003.
Values sent between devices are 32-bit elements; how exact they have to be, the bound alone decides.
A program may use at most 64 MiB of HBM per device.

v0:
```python
import math
import jax
import jax.numpy as jnp
from jax import lax
from jax.sharding import PartitionSpec as P

ITERS = 8
epsilon = 0.05


def joined(value, axis, join):
    pieces = jax.tree.map(lambda part: lax.all_gather(part, axis), value)
    head = jax.tree.map(lambda part: part[0], pieces)
    tail = jax.tree.map(lambda part: part[1:], pieces)
    total, _ = lax.scan(lambda total, piece: (join(total, piece), None), head, tail)
    return total


def pair_cost(points, observed):
    feature_count = points.shape[0]
    sq_points = jnp.sum(points * points, 0)
    sq_observed = jnp.sum(observed * observed, 0)
    inner_products = lax.dot_general(
        points,
        observed,
        (((0,), (0,)), ((), ())),
        precision=lax.Precision.HIGHEST,
        preferred_element_type=jnp.float32,
    )
    return (sq_points[:, None] + sq_observed[None, :] - 2.0 * inner_products) / feature_count


def lse_combine(first, second):
    new_top = jnp.maximum(first[0], second[0])
    return (
        new_top,
        first[1] * jnp.exp(first[0] - new_top) + second[1] * jnp.exp(second[0] - new_top),
    )


def on_device(sim_points, obs_points, sim_logw, obs_logw):
    row_count = lax.axis_size("row")
    obs_dev = obs_points.shape[1]
    total_sim = sim_points.shape[1] * row_count
    total_obs = obs_dev * row_count * lax.axis_size("col")
    observed, logw_all = (
        lax.all_gather(obs_points, "row", axis=1, tiled=True),
        lax.all_gather(obs_logw, "row", axis=0, tiled=True),
    )
    log_a = sim_logw - math.log(total_sim)
    log_b_all = logw_all - math.log(total_obs)
    own_index = lax.axis_index("row")
    resident = pair_cost(sim_points, observed)

    def costs():
        return resident

    potential_g = jnp.zeros((observed.shape[1],), jnp.float32)
    potential_g_own = jnp.zeros((obs_dev,), jnp.float32)
    potential_f = jnp.zeros((sim_points.shape[1],), jnp.float32)
    for iteration in range(ITERS):
        scores = (potential_g[None, :] - costs()) / epsilon
        row_top = jnp.max(scores, 1)
        row_mass = jnp.sum(jnp.exp(scores - row_top[:, None]), 1)
        row_top, row_mass = joined((row_top, row_mass), "col", lse_combine)
        potential_f = epsilon * log_a - epsilon * (row_top + jnp.log(row_mass))
        scores = (potential_f[:, None] - costs()) / epsilon
        col_top = jnp.max(scores, 0)
        col_mass = jnp.sum(jnp.exp(scores - col_top[None, :]), 0)
        col_top, col_mass = joined((col_top, col_mass), "row", lse_combine)
        potential_g = epsilon * log_b_all - epsilon * (col_top + jnp.log(col_mass))
        potential_g_own = lax.dynamic_slice_in_dim(potential_g, own_index * obs_dev, obs_dev)
    costs_tile = costs()
    transport = jnp.exp((potential_f[:, None] + potential_g[None, :] - costs_tile) / epsilon)
    total_cost = lax.psum(jnp.sum(transport * costs_tile), ("row", "col"))
    return (potential_f, potential_g_own, jnp.reshape(total_cost, (1,)))


def solution(mesh):
    in_specs = (P(None, "row"), P(None, ("row", "col")), P("row"), P(("row", "col")))
    out_specs = (P("row"), P(("row", "col")), P())
    return jax.shard_map(
        on_device, mesh=mesh, in_specs=in_specs, out_specs=out_specs, check_vma=False
    )
```

profile of v0, /device:TPU:14, one launch (start us, length us, event | category | flops | bytes accessed | tf_op | source)
XLA Modules:
  0.0 770.5 jit_solution(11684991094862416299)
XLA Ops:
  0.6 31.2 %all_gather.199 = f32[64,2048]{1,0:T(8,128)S(1)} all-gather(f32[64,128]{1,0:T(8,128)} %param.21), channel_id=1, replica_groups=mesh['row'=16,'col'=2] {'row'}, dimensions={1}, use_global_device_ids=true | all-gather | bytes 557056 | tf_op jit(solution)/shard_map/all_gather | solution.py:47
  32.8 3.2 fusion.2
  35.9 38.6 %all-gather.32 = f32[16,1,128]{2,1,0:T(1,128)S(1)} all-gather(f32[1,1,128]{2,1,0:T(1,128)S(1)} %bitcast.173), channel_id=1, replica_groups=mesh['row'=16,'col'=2] {'row'}, dimensions={0}, use_global_device_ids=true | all-gather | bytes 8704 | tf_op jit(solution)/shard_map/all_gather | solution.py:48
  75.1 1.8 all-gather.34
  76.9 1.8 all-gather.33
  79.0 36.1 %all-gather.2 = f32[32768]{0:T(1024)S(1)} all-gather(f32[2048]{0:T(1024)S(1)} %fusion.3), channel_id=4, replica_groups=mesh['row'=16,'col'=2] {'row'}, dimensions={0}, use_global_device_ids=true | all-gather | bytes 139264 | tf_op jit(solution)/shard_map/all_gather | solution.py:12
  115.6 38.2 %all-gather.3 = f32[32768]{0:T(1024)S(1)} all-gather(f32[2048]{0:T(1024)S(1)} %exponential_reduce_fusion.14), channel_id=5, replica_groups=mesh['row'=16,'col'=2] {'row'}, dimensions={0}, use_global_device_ids=true | all-gather | bytes 139264 | tf_op jit(solution)/shard_map/all_gather | solution.py:12
  155.7 1.8 all-gather.36
  159.6 36.1 %all-gather.6 = f32[32768]{0:T(1024)S(1)} all-gather(f32[2048]{0:T(1024)S(1)} %fusion.5), channel_id=8, replica_groups=mesh['row'=16,'col'=2] {'row'}, dimensions={0}, use_global_device_ids=true | all-gather | bytes 139264 | tf_op jit(solution)/shard_map/all_gather | solution.py:12
  196.2 38.2 %all-gather.7 = f32[32768]{0:T(1024)S(1)} all-gather(f32[2048]{0:T(1024)S(1)} %exponential_reduce_fusion.12), channel_id=9, replica_groups=mesh['row'=16,'col'=2] {'row'}, dimensions={0}, use_global_device_ids=true | all-gather | bytes 139264 | tf_op jit(solution)/shard_map/all_gather | solution.py:12
  236.2 1.8 all-gather.38
  238.0 1.8 all-gather.37
  240.1 36.1 %all-gather.10 = f32[32768]{0:T(1024)S(1)} all-gather(f32[2048]{0:T(1024)S(1)} %fusion.7), channel_id=12, replica_groups=mesh['row'=16,'col'=2] {'row'}, dimensions={0}, use_global_device_ids=true | all-gather | bytes 139264 | tf_op jit(solution)/shard_map/all_gather | solution.py:12
  276.8 38.2 %all-gather.11 = f32[32768]{0:T(1024)S(1)} all-gather(f32[2048]{0:T(1024)S(1)} %exponential_reduce_fusion.10), channel_id=13, replica_groups=mesh['row'=16,'col'=2] {'row'}, dimensions={0}, use_global_device_ids=true | all-gather | bytes 139264 | tf_op jit(solution)/shard_map/all_gather | solution.py:12
  316.8 1.8 all-gather.40
  318.6 1.8 all-gather.39
  320.7 36.1 %all-gather.14 = f32[32768]{0:T(1024)S(1)} all-gather(f32[2048]{0:T(1024)S(1)} %fusion.9), channel_id=16, replica_groups=mesh['row'=16,'col'=2] {'row'}, dimensions={0}, use_global_device_ids=true | all-gather | bytes 139264 | tf_op jit(solution)/shard_map/all_gather | solution.py:12
  357.3 38.2 %all-gather.15 = f32[32768]{0:T(1024)S(1)} all-gather(f32[2048]{0:T(1024)S(1)} %exponential_reduce_fusion.8), channel_id=17, replica_groups=mesh['row'=16,'col'=2] {'row'}, dimensions={0}, use_global_device_ids=true | all-gather | bytes 139264 | tf_op jit(solution)/shard_map/all_gather | solution.py:12
  397.4 1.8 all-gather.42
  401.3 36.1 %all-gather.18 = f32[32768]{0:T(1024)S(1)} all-gather(f32[2048]{0:T(1024)S(1)} %fusion.11), channel_id=20, replica_groups=mesh['row'=16,'col'=2] {'row'}, dimensions={0}, use_global_device_ids=true | all-gather | bytes 139264 | tf_op jit(solution)/shard_map/all_gather | solution.py:12
  437.9 38.3 %all-gather.19 = f32[32768]{0:T(1024)S(1)} all-gather(f32[2048]{0:T(1024)S(1)} %exponential_reduce_fusion.6), channel_id=21, replica_groups=mesh['row'=16,'col'=2] {'row'}, dimensions={0}, use_global_device_ids=true | all-gather | bytes 139264 | tf_op jit(solution)/shard_map/all_gather | solution.py:12
  478.1 1.8 all-gather.44
  482.0 36.2 %all-gather.22 = f32[32768]{0:T(1024)S(1)} all-gather(f32[2048]{0:T(1024)S(1)} %fusion.13), channel_id=24, replica_groups=mesh['row'=16,'col'=2] {'row'}, dimensions={0}, use_global_device_ids=true | all-gather | bytes 139264 | tf_op jit(solution)/shard_map/all_gather | solution.py:12
  518.8 38.1 %all-gather.23 = f32[32768]{0:T(1024)S(1)} all-gather(f32[2048]{0:T(1024)S(1)} %exponential_reduce_fusion.4), channel_id=25, replica_groups=mesh['row'=16,'col'=2] {'row'}, dimensions={0}, use_global_device_ids=true | all-gather | bytes 139264 | tf_op jit(solution)/shard_map/all_gather | solution.py:12
  558.7 1.8 all-gather.46
  560.5 1.8 all-gather.45
  562.6 36.2 %all-gather.26 = f32[32768]{0:T(1024)S(1)} all-gather(f32[2048]{0:T(1024)S(1)} %fusion.15), channel_id=28, replica_groups=mesh['row'=16,'col'=2] {'row'}, dimensions={0}, use_global_device_ids=true | all-gather | bytes 139264 | tf_op jit(solution)/shard_map/all_gather | solution.py:12
  599.3 38.1 %all-gather.27 = f32[32768]{0:T(1024)S(1)} all-gather(f32[2048]{0:T(1024)S(1)} %exponential_reduce_fusion.2), channel_id=29, replica_groups=mesh['row'=16,'col'=2] {'row'}, dimensions={0}, use_global_device_ids=true | all-gather | bytes 139264 | tf_op jit(solution)/shard_map/all_gather | solution.py:12
  639.3 1.8 all-gather.48
  643.2 36.2 %all-gather.30 = f32[32768]{0:T(1024)S(1)} all-gather(f32[2048]{0:T(1024)S(1)} %fusion.17), channel_id=32, replica_groups=mesh['row'=16,'col'=2] {'row'}, dimensions={0}, use_global_device_ids=true | all-gather | bytes 139264 | tf_op jit(solution)/shard_map/all_gather | solution.py:12
  679.9 38.1 %all-gather.31 = f32[32768]{0:T(1024)S(1)} all-gather(f32[2048]{0:T(1024)S(1)} %exponential_reduce_fusion), channel_id=33, replica_groups=mesh['row'=16,'col'=2] {'row'}, dimensions={0}, use_global_device_ids=true | all-gather | bytes 139264 | tf_op jit(solution)/shard_map/all_gather | solution.py:12
  721.2 49.3 %psum.7 = f32[1]{0:T(128)} all-reduce(f32[1]{0:T(128)} %bitcast.66), channel_id=1, replica_groups=mesh['row'=16,'col'=2] {'row','col'}, use_global_device_ids=true, to_apply=%region_51.52 | all-reduce | flops 1 | bytes 8 | tf_op jit(solution)/shard_map/psum | solution.py:75
  (374 shorter events, 35.1 us)
Async XLA Ops:
  31.8 4.1 copy-start.2
  32.8 45.9 %copy-start = (f32[256]{0:T(256)S(1)}, f32[256]{0:T(256)}, u32[]{:S(2)}) copy-start(f32[256]{0:T(256)} %param.22) | copy-start | bytes 3076
  642.9 76.8 %copy-start.1 = (f32[256]{0:T(256)}, f32[256]{0:T(256)S(1)}, u32[]{:S(2)}) copy-start(f32[256]{0:T(256)S(1)} %multiply_subtract_fusion.8) | copy-start | bytes 3076
where the time goes:
time: 771 us
  blocking collectives  742 us (96%)
  other arithmetic  17 us (2%)
    all_gather x32, blocking collectives, joined(): pieces = jax.tree.map(lambda part: lax.all_gather(part, axis), value)  623 us
    psum x1, blocking collectives, on_device(): total_cost = lax.psum(jnp.sum(transport * costs_tile), ('row', 'col'))  49.3 us
    all_gather x1, blocking collectives, on_device(): lax.all_gather(obs_logw, 'row', axis=0, tiled=True)  38.6 us
    all_gather x1, blocking collectives, on_device(): lax.all_gather(obs_points, 'row', axis=1, tiled=True)  31.2 us

commit v1 on v0

--- a/solution.py
+++ b/solution.py
@@ -6,6 +6,17 @@
 
 ITERS = 8
 epsilon = 0.05
+
+
+def collect(shard, axis, dim):
+    ways = lax.axis_size(axis)
+    pieces = [shard]
+    for far in range(1, ways):
+        pieces.append(
+            lax.ppermute(pieces[far - 1], axis, [(d, (d - 1) % ways) for d in range(ways)])
+        )
+    line = jnp.concatenate(pieces, axis=dim)
+    return jnp.roll(line, lax.axis_index(axis) * shard.shape[dim], axis=dim)
 
 
 def joined(value, axis, join):
@@ -44,7 +55,7 @@
     total_sim = sim_points.shape[1] * row_count
     total_obs = obs_dev * row_count * lax.axis_size("col")
     observed, logw_all = (
-        lax.all_gather(obs_points, "row", axis=1, tiled=True),
+        collect(obs_points, "row", 1),
         lax.all_gather(obs_logw, "row", axis=0, tiled=True),
     )
     log_a = sim_logw - math.log(total_sim)

time: 771 us -> 842 us (1.092)
  waiting for transfers between devices: 0 us -> 76.7 us
  blocking collectives: 742 us -> 728 us
    ppermute x0 -> x15, waiting for transfers between devices: none -> 76.7 us  [collect(): lax.ppermute(pieces[far - 1], axis, [(d, (d - 1) % ways) for d in range(w...]
    all_gather x1 -> x0, blocking collectives: 31.2 us -> none  [on_device(): lax.all_gather(obs_points, 'row', axis=1, tiled=True)]
    all_gather x32, blocking collectives: 623 us -> 648 us  [joined(): pieces = jax.tree.map(lambda part: lax.all_gather(part, axis), value)]
  transfers between devices with their start and end apart: 0 -> 15, of which waited for: 0 -> 14; matrix products, arithmetic and copies ran while one was open for 0% -> 0% of each run, Pallas kernels for 0% -> 0%
where the time goes in v1:
time: 842 us
  blocking collectives  728 us (86%)
  waiting for transfers between devices  76.7 us (9%)
  other arithmetic  19.9 us (2%)
    all_gather x32, blocking collectives, joined(): pieces = jax.tree.map(lambda part: lax.all_gather(part, axis), value)  648 us
    ppermute x15, waiting for transfers between devices, collect(): lax.ppermute(pieces[far - 1], axis, [(d, (d - 1) % ways) for d in range(w...  76.7 us
    psum x1, blocking collectives, on_device(): total_cost = lax.psum(jnp.sum(transport * costs_tile), ('row', 'col'))  49.4 us
    all_gather x1, blocking collectives, on_device(): lax.all_gather(obs_logw, 'row', axis=0, tiled=True)  30.8 us
  transfers between devices with their start and end apart: 15, of which 14 were waited for; matrix products, arithmetic and copies ran while one was open for 0% of the time, Pallas kernels for 0%

profile of v1, /device:TPU:14, one launch (start us, length us, event | category | flops | bytes accessed | tf_op | source)
XLA Modules:
  0.0 841.5 jit_solution(17609358861868873248)
XLA Ops:
  2.1 30.8 %all-gather.32 = f32[16,1,128]{2,1,0:T(1,128)S(1)} all-gather(f32[1,1,128]{2,1,0:T(1,128)} %bitcast.178), channel_id=1, replica_groups=mesh['row'=16,'col'=2] {'row'}, dimensions={0}, use_global_device_ids=true | all-gather | bytes 8704 | tf_op jit(solution)/shard_map/all_gather | solution.py:59
  34.3 5.1 collective-permute-done.1
  40.9 4.2 collective-permute-done.2
  45.7 5.1 collective-permute-done.3
  50.8 5.7 collective-permute-done.4
  56.5 5.7 collective-permute-done.5
  62.3 5.7 collective-permute-done.6
  68.0 5.7 collective-permute-done.7
  73.7 5.7 collective-permute-done.8
  79.4 5.7 collective-permute-done.9
  85.1 5.9 collective-permute-done.10
  91.1 5.7 collective-permute-done.11
  96.8 5.7 collective-permute-done.12
  102.5 5.7 collective-permute-done.13
  108.9 5.0 collective-permute-done.14
  122.6 57.7 %all-gather.2 = f32[32768]{0:T(1024)S(1)} all-gather(f32[2048]{0:T(1024)S(1)} %fusion.4), channel_id=4, replica_groups=mesh['row'=16,'col'=2] {'row'}, dimensions={0}, use_global_device_ids=true | all-gather | bytes 139264 | tf_op jit(solution)/shard_map/all_gather | solution.py:23
  180.3 41.7 %all-gather.3 = f32[32768]{0:T(1024)S(1)} all-gather(f32[2048]{0:T(1024)S(1)} %exponential_reduce_fusion.14), channel_id=5, replica_groups=mesh['row'=16,'col'=2] {'row'}, dimensions={0}, use_global_device_ids=true | all-gather | bytes 139264 | tf_op jit(solution)/shard_map/all_gather | solution.py:23
  228.7 36.2 %all-gather.6 = f32[32768]{0:T(1024)S(1)} all-gather(f32[2048]{0:T(1024)S(1)} %fusion.6), channel_id=8, replica_groups=mesh['row'=16,'col'=2] {'row'}, dimensions={0}, use_global_device_ids=true | all-gather | bytes 139264 | tf_op jit(solution)/shard_map/all_gather | solution.py:23
  264.9 38.1 %all-gather.7 = f32[32768]{0:T(1024)S(1)} all-gather(f32[2048]{0:T(1024)S(1)} %exponential_reduce_fusion.12), channel_id=9, replica_groups=mesh['row'=16,'col'=2] {'row'}, dimensions={0}, use_global_device_ids=true | all-gather | bytes 139264 | tf_op jit(solution)/shard_map/all_gather | solution.py:23
  309.7 36.1 %all-gather.10 = f32[32768]{0:T(1024)S(1)} all-gather(f32[2048]{0:T(1024)S(1)} %fusion.8), channel_id=12, replica_groups=mesh['row'=16,'col'=2] {'row'}, dimensions={0}, use_global_device_ids=true | all-gather | bytes 139264 | tf_op jit(solution)/shard_map/all_gather | solution.py:23
  345.9 38.3 %all-gather.11 = f32[32768]{0:T(1024)S(1)} all-gather(f32[2048]{0:T(1024)S(1)} %exponential_reduce_fusion.10), channel_id=13, replica_groups=mesh['row'=16,'col'=2] {'row'}, dimensions={0}, use_global_device_ids=true | all-gather | bytes 139264 | tf_op jit(solution)/shard_map/all_gather | solution.py:23
  390.9 36.2 %all-gather.14 = f32[32768]{0:T(1024)S(1)} all-gather(f32[2048]{0:T(1024)S(1)} %fusion.10), channel_id=16, replica_groups=mesh['row'=16,'col'=2] {'row'}, dimensions={0}, use_global_device_ids=true | all-gather | bytes 139264 | tf_op jit(solution)/shard_map/all_gather | solution.py:23
  427.1 38.1 %all-gather.15 = f32[32768]{0:T(1024)S(1)} all-gather(f32[2048]{0:T(1024)S(1)} %exponential_reduce_fusion.8), channel_id=17, replica_groups=mesh['row'=16,'col'=2] {'row'}, dimensions={0}, use_global_device_ids=true | all-gather | bytes 139264 | tf_op jit(solution)/shard_map/all_gather | solution.py:23
  471.9 36.2 %all-gather.18 = f32[32768]{0:T(1024)S(1)} all-gather(f32[2048]{0:T(1024)S(1)} %fusion.12), channel_id=20, replica_groups=mesh['row'=16,'col'=2] {'row'}, dimensions={0}, use_global_device_ids=true | all-gather | bytes 139264 | tf_op jit(solution)/shard_map/all_gather | solution.py:23
  508.0 38.1 %all-gather.19 = f32[32768]{0:T(1024)S(1)} all-gather(f32[2048]{0:T(1024)S(1)} %exponential_reduce_fusion.6), channel_id=21, replica_groups=mesh['row'=16,'col'=2] {'row'}, dimensions={0}, use_global_device_ids=true | all-gather | bytes 139264 | tf_op jit(solution)/shard_map/all_gather | solution.py:23
  552.8 36.2 %all-gather.22 = f32[32768]{0:T(1024)S(1)} all-gather(f32[2048]{0:T(1024)S(1)} %fusion.14), channel_id=24, replica_groups=mesh['row'=16,'col'=2] {'row'}, dimensions={0}, use_global_device_ids=true | all-gather | bytes 139264 | tf_op jit(solution)/shard_map/all_gather | solution.py:23
  589.0 38.1 %all-gather.23 = f32[32768]{0:T(1024)S(1)} all-gather(f32[2048]{0:T(1024)S(1)} %exponential_reduce_fusion.4), channel_id=25, replica_groups=mesh['row'=16,'col'=2] {'row'}, dimensions={0}, use_global_device_ids=true | all-gather | bytes 139264 | tf_op jit(solution)/shard_map/all_gather | solution.py:23
  633.8 36.2 %all-gather.26 = f32[32768]{0:T(1024)S(1)} all-gather(f32[2048]{0:T(1024)S(1)} %fusion.16), channel_id=28, replica_groups=mesh['row'=16,'col'=2] {'row'}, dimensions={0}, use_global_device_ids=true | all-gather | bytes 139264 | tf_op jit(solution)/shard_map/all_gather | solution.py:23
  670.0 38.1 %all-gather.27 = f32[32768]{0:T(1024)S(1)} all-gather(f32[2048]{0:T(1024)S(1)} %exponential_reduce_fusion.2), channel_id=29, replica_groups=mesh['row'=16,'col'=2] {'row'}, dimensions={0}, use_global_device_ids=true | all-gather | bytes 139264 | tf_op jit(solution)/shard_map/all_gather | solution.py:23
  714.8 36.2 %all-gather.30 = f32[32768]{0:T(1024)S(1)} all-gather(f32[2048]{0:T(1024)S(1)} %fusion.18), channel_id=32, replica_groups=mesh['row'=16,'col'=2] {'row'}, dimensions={0}, use_global_device_ids=true | all-gather | bytes 139264 | tf_op jit(solution)/shard_map/all_gather | solution.py:23
  751.0 38.1 %all-gather.31 = f32[32768]{0:T(1024)S(1)} all-gather(f32[2048]{0:T(1024)S(1)} %exponential_reduce_fusion), channel_id=33, replica_groups=mesh['row'=16,'col'=2] {'row'}, dimensions={0}, use_global_device_ids=true | all-gather | bytes 139264 | tf_op jit(solution)/shard_map/all_gather | solution.py:23
  791.6 49.4 %psum.7 = f32[1]{0:T(128)} all-reduce(f32[1]{0:T(128)} %bitcast.67), channel_id=1, replica_groups=mesh['row'=16,'col'=2] {'row','col'}, use_global_device_ids=true, to_apply=%region_51.52 | all-reduce | flops 1 | bytes 8 | tf_op jit(solution)/shard_map/psum | solution.py:86
  (435 shorter events, 67.4 us)
Async XLA Ops:
  0.6 114.3 %copy-start = (f32[64,256]{1,0:T(8,128)S(1)}, f32[64,256]{1,0:T(8,128)}, u32[]{:S(2)}) copy-start(f32[64,256]{1,0:T(8,128)} %param.20) | copy-start | bytes 196612
  0.6 33.0 %collective-permute-start = (f32[64,128]{1,0:T(8,128)}, f32[64,128]{1,0:T(8,128)S(1)}, u32[]{:S(2)}, u32[]{:S(2)}) collective-permute-start(f32[64,128]{1,0:T(8,128)} %param.21), channel_id=1, source_target_pairs={{0,30},{2,0},{4,2},{6,4},{8,6},{10,8},{12,10},{14,12},{16,14},{18,... | collective-permute-start | bytes 98312 | tf_op jit(solution)/shard_map/ppermute | solution.py:16
  33.7 5.7 collective-permute-start.1
  39.4 5.7 collective-permute-start.2
  45.1 5.7 collective-permute-start.3
  50.8 5.7 collective-permute-start.4
  56.5 5.7 collective-permute-start.5
  62.2 5.7 collective-permute-start.6
  68.0 5.7 collective-permute-start.7
  73.7 5.7 collective-permute-start.8
  79.4 5.7 collective-permute-start.9
  85.1 5.9 collective-permute-start.10
  91.0 5.7 collective-permute-start.11
  96.8 5.7 collective-permute-start.12
  102.5 5.7 collective-permute-start.13
  108.2 5.7 collective-permute-start.14
  114.9 6.5 copy-start.1
  713.6 76.5 %copy-start.2 = (f32[256]{0:T(256)}, f32[256]{0:T(256)S(1)}, u32[]{:S(2)}) copy-start(f32[256]{0:T(256)S(1)} %multiply_subtract_fusion.8) | copy-start | bytes 3076
